TPU v7x, 32 devices: a whole 2x2x4 slice. The times are simulated.
32 devices in a mesh: ia: 2 (over y), ja: 4 (over z), ka: 4 (over x, core).
Axes of the slice: x: 2, y: 2, z: 4, core: 2. Of those that a mesh axis runs over, the one named last changes fastest.
Arguments:
- blocks: bfloat16 [256, 64, 4096], P(('ia', 'ja', 'ka')), may hold values from -12 to 12
- coords: int32 [256, 3], P(('ia', 'ja', 'ka')), may hold values from 0 to 63, as said below
- factor_one: float32 [2048, 512], P('ia'), may hold values from -1.2 to 1.2
- factor_two: float32 [4096, 512], P('ja'), may hold values from -1.2 to 1.2
- factor_three: float32 [4096, 512], P('ka'), may hold values from -1.2 to 1.2
Outputs:
- swept_one: float32 [2048, 512], P('ia')
- swept_two: float32 [4096, 512], P('ja')
- swept_three: float32 [4096, 512], P('ka')
Inputs may be any that keep to these rules, and one draw needn't show every extreme that they name: Row n of coords holds the three block coordinates of block n. The 8 rows of one device of ia+ja+ka (aligned blocks of 8 rows, devices in the order ia, ja, ka) have their second coordinate within that device's ja range (16 * ja to 16 * ja + 15) and their third within its ka range; at most 8 of them have a first coordinate within any one index of ia's range of 16; in every group of devices that share ja and ka, some index of ia receives exactly 8 from each device of the group. The same block may be listed more than once.
All inputs are finite; a program needn't handle non-finite values.
Results may differ from a plain program's by a relative error of at most 0.0028.
Values may be sent and summed in bfloat16 or wider, within the bound.
A program may use at most 64 MiB of HBM per device.

v0:
```python
import jax
import jax.numpy as jnp
from jax import lax
from jax.sharding import PartitionSpec as P

STEP_SIZE = 0.01
einsum_forms = (
    ("qk,rk->qrk", "pk,qrk->pqr", "pqr,qrk->pk"),
    ("pk,rk->prk", "qk,prk->pqr", "pqr,prk->qk"),
    ("pk,qk->pqk", "rk,pqk->pqr", "pqr,pqk->rk"),
)
other_modes = ((1, 2), (0, 2), (0, 1))


def block_gradient(cube, rows, mode):
    first, second = other_modes[mode]
    outer_form, model_form, grad_form = einsum_forms[mode]
    khatri = jnp.einsum(
        outer_form, rows[first].astype(jnp.float32), rows[second].astype(jnp.float32)
    ).astype(jnp.bfloat16)
    model = jnp.einsum(model_form, rows[mode], khatri, preferred_element_type=jnp.float32)
    misfit = (cube.astype(jnp.float32) - model).astype(jnp.bfloat16)
    return jnp.einsum(grad_form, misfit, khatri, preferred_element_type=jnp.float32)


def accumulate(blocks, coords, factors, starts, live, mode, height):
    edge = blocks.shape[1]
    width = factors[0].shape[1]

    def visit(index, total):

        def add(running):
            place = coords[index]
            rows = tuple(
                (
                    lax.dynamic_slice_in_dim(factors[f], place[f] * edge - starts[f], edge, 0)
                    for f in range(3)
                )
            )
            cube = blocks[index].reshape(edge, edge, edge)
            term = block_gradient(cube, rows, mode)
            offset = place[mode] * edge - starts[mode]
            current = lax.dynamic_slice_in_dim(running, offset, edge, 0)
            return lax.dynamic_update_slice_in_dim(running, current + term, offset, 0)

        return lax.cond(live[index], add, lambda running: running, total)

    empty = jnp.zeros((height, width), jnp.float32)
    return lax.fori_loop(0, blocks.shape[0], visit, empty)


def block_slots(coords, count, per_pair, held_rows):
    target = coords[:, 0] // held_rows
    same = target[:, None] == target[None, :]
    earlier = jnp.arange(count)[None, :] < jnp.arange(count)[:, None]
    before = jnp.sum((same & earlier).astype(jnp.int32), axis=1)
    return target * per_pair + before


def serve_rows(incoming, factor, edge, held_rows):
    width = factor.shape[1]
    within = incoming - lax.axis_index("ia") * held_rows
    safe_rows = jnp.clip(within, 0, held_rows - 1)
    picked = factor.astype(jnp.bfloat16).reshape(held_rows, edge, width)[safe_rows]
    return lax.all_to_all(picked, "ia", split_axis=0, concat_axis=0, tiled=True)


def per_device(blocks, coords, factor_one, factor_two, factor_three):
    edge = blocks.shape[1]
    count = blocks.shape[0]
    groups = lax.axis_size("ia")
    span_one = factor_one.shape[0]
    span_two = factor_two.shape[0]
    span_three = factor_three.shape[0]
    width = factor_one.shape[1]
    held_rows = span_one // edge
    per_pair = max(2, 2 * count // groups)
    start_two = lax.axis_index("ja") * span_two
    start_three = lax.axis_index("ka") * span_three
    slot = block_slots(coords, count, per_pair, held_rows)
    all_slots = groups * per_pair
    wanted = jnp.full((all_slots,), -1, jnp.int32).at[slot].set(coords[:, 0])
    incoming = lax.all_to_all(wanted, "ia", split_axis=0, concat_axis=0, tiled=True)
    fetched = serve_rows(incoming, factor_one, edge, held_rows).reshape(all_slots * edge, width)
    places = coords.at[:, 0].set(slot)
    live = jnp.ones((count,), jnp.bool_)
    slot_terms = accumulate(
        blocks,
        places,
        (fetched, factor_two.astype(jnp.bfloat16), factor_three.astype(jnp.bfloat16)),
        (0, start_two, start_three),
        live,
        0,
        all_slots * edge,
    )
    returned = lax.all_to_all(
        slot_terms.reshape(all_slots, edge, width), "ia", split_axis=0, concat_axis=0, tiled=True
    )
    within = incoming - lax.axis_index("ia") * held_rows
    selector = (within[None, :] == jnp.arange(held_rows)[:, None]).astype(jnp.float32)
    first_part = jnp.dot(
        selector,
        returned.reshape(all_slots, edge * width),
        precision=lax.Precision.HIGHEST,
        preferred_element_type=jnp.float32,
    ).reshape(span_one, width)
    first_part = lax.psum(first_part, ("ja", "ka"))
    factor_one = factor_one + STEP_SIZE * first_part
    first_rows = serve_rows(incoming, factor_one, edge, held_rows).reshape(
        groups * per_pair * edge, width
    )
    first_start = 0
    second_part = accumulate(
        blocks,
        places,
        (first_rows, factor_two.astype(jnp.bfloat16), factor_three.astype(jnp.bfloat16)),
        (first_start, start_two, start_three),
        live,
        1,
        span_two,
    )
    second_part = lax.psum(second_part, ("ia", "ka"))
    factor_two = factor_two + STEP_SIZE * second_part
    third_part = accumulate(
        blocks,
        places,
        (first_rows, factor_two.astype(jnp.bfloat16), factor_three.astype(jnp.bfloat16)),
        (first_start, start_two, start_three),
        live,
        2,
        span_three,
    )
    third_part = lax.psum(third_part, ("ia", "ja"))
    factor_three = factor_three + STEP_SIZE * third_part
    return (factor_one, factor_two, factor_three)


def solution(mesh):
    in_specs = (
        P(("ia", "ja", "ka"), None, None),
        P(("ia", "ja", "ka"), None),
        P("ia", None),
        P("ja", None),
        P("ka", None),
    )
    out_specs = (P("ia", None), P("ja", None), P("ka", None))
    return jax.shard_map(
        per_device, mesh=mesh, in_specs=in_specs, out_specs=out_specs, check_vma=False
    )
```

profile of v0, /device:TPU:0, one launch (start us, length us, event | category | flops | bytes accessed | tf_op | source)
XLA Modules:
  0.0 621.7 jit_solution(2798835930513432250)
XLA Ops:
  10.6 4.3 all-to-all-start
  27.9 8.9 %all-to-all-done.1 = bf16[16,64,512]{2,1,0:T(8,128)(2,1)S(1)} async-done(((bf16[16,64,512]{2,1,0:T(8,128)(2,1)}), bf16[16,64,512]{2,1,0:T(8,128)(2,1)S(1)}, u32[]{:S(2)}, u32[]{:S(2)}) %all-to-all-start.1) | async-done | bytes 1048608 | tf_op jit(solution)/shard_map/all_to_all | solution.py:65
  38.3 86.3 %while.40 = (s32[]{:T(128)}, f32[1024,512]{1,0:T(8,128)}, s32[8,3]{0,1:T(4,128)S(1)}, bf16[8,64,4096]{2,1,0:T(8,128)(2,1)}, bf16[1024,512]{1,0:T(8,128)(2,1)S(1)...) while((s32[]{:T(128)}, f32[1024,512]{1,0:T(8,128)}, ...), condition=%wide.region_4.5_spmd, body=%wide.region_3.4_spmd.sunk | while | flops 546144256 | bytes 15402399 | solution.py:49
  44.1 5.0 fusion.118
  54.8 5.0 fusion.118
  65.6 5.0 fusion.118
  76.4 5.0 fusion.118
  87.2 5.0 fusion.118
  98.0 5.0 fusion.118
  108.8 5.0 fusion.118
  119.6 5.0 fusion.118
  128.5 23.1 %all-to-all-done.2 = f32[16,64,512]{2,1,0:T(8,128)S(1)} async-done(((f32[16,64,512]{2,1,0:T(8,128)}), f32[16,64,512]{2,1,0:T(8,128)S(1)}, u32[]{:S(2)}, u32[]{:S(2)}) %all-to-all-start.2) | async-done | bytes 2097184 | tf_op jit(solution)/shard_map/all_to_all | solution.py:96
  155.5 98.7 %all-reduce.4.cloned.1.call-done = f32[1024,512]{1,0:T(8,128)} async-done(((f32[1024,512]{1,0:T(8,128)}), f32[1024,512]{1,0:T(8,128)}) %all-reduce.4.cloned.1.call-update) | async-done | bytes 2097168 | tf_op jit(solution)/shard_map/psum | solution.py:107
  259.3 4.4 all-to-all-start.3
  263.9 12.9 %all-to-all-done.3 = bf16[16,64,512]{2,1,0:T(8,128)(2,1)} async-done(((bf16[16,64,512]{2,1,0:T(8,128)(2,1)}), bf16[16,64,512]{2,1,0:T(8,128)(2,1)}, u32[]{:S(2)}, u32[]{:S(2)}) %all-to-all-start.3) | async-done | bytes 1048608 | tf_op jit(solution)/shard_map/all_to_all | solution.py:65
  278.4 92.2 %while.41 = (s32[]{:T(128)}, f32[1024,512]{1,0:T(8,128)}, s32[8,3]{0,1:T(4,128)S(1)}, s32[]{:T(128)}, bf16[8,64,4096]{2,1,0:T(8,128)(2,1)}, /*index=5*/s32[]{:T(...) while((s32[]{:T(128)}, f32[1024,512]{1,0:T(8,128)}, ...), condition=%wide.region_7.8_spmd, body=%wide.region_6.7_spmd.sunk | while | flops 546144256 | bytes 9110887 | solution.py:49
  285.6 4.4 fusion.123
  297.1 4.4 fusion.123
  308.6 4.4 fusion.123
  320.1 4.4 fusion.123
  331.6 4.4 fusion.123
  343.2 4.4 fusion.123
  354.7 4.4 fusion.123
  366.2 4.4 fusion.123
  370.6 59.9 %all-reduce.6.cloned.1.call-done = f32[1024,512]{1,0:T(8,128)} async-done(((f32[1024,512]{1,0:T(8,128)}), f32[1024,512]{1,0:T(8,128)}) %all-reduce.6.cloned.1.call-update) | async-done | bytes 2097168 | tf_op jit(solution)/shard_map/psum | solution.py:122
  435.6 74.6 %while.42 = (s32[]{:T(128)}, f32[1024,512]{1,0:T(8,128)}, s32[8,3]{0,1:T(4,128)S(1)}, s32[]{:T(128)}, bf16[8,64,4096]{2,1,0:T(8,128)(2,1)}, /*index=5*/s32[]{:T(...) while((s32[]{:T(128)}, f32[1024,512]{1,0:T(8,128)}, ...), condition=%wide.region_10.11_spmd, body=%wide.region_9.10_spmd.sunk | while | flops 546144256 | bytes 15402399 | solution.py:49
  469.1 3.8 fusion.128
  478.4 3.8 fusion.128
  487.7 3.8 fusion.128
  497.0 3.8 fusion.128
  506.4 3.8 fusion.128
  510.2 101.5 %all-reduce.8.cloned.1.call-done = f32[1024,512]{1,0:T(8,128)} async-done(((f32[1024,512]{1,0:T(8,128)}), f32[1024,512]{1,0:T(8,128)}) %all-reduce.8.cloned.1.call-update) | async-done | bytes 2097168 | tf_op jit(solution)/shard_map/psum | solution.py:133
  (240 shorter events, 152.5 us)
Async XLA Ops:
  10.6 8.0 %all-to-all-start = ((s32[2,8,1]{1,2,0:T(1,128)}), s32[2,8,1]{1,2,0:T(1,128)S(1)}, u32[]{:S(2)}, u32[]{:S(2)}) async-start(s32[2,8,1]{1,2,0:T(1,128)} %bitcast.29), calls=%async_computation | async-start | bytes 2048 | tf_op jit(solution)/shard_map/all_to_all | solution.py:83
  20.3 16.5 %all-to-all-start.1 = ((bf16[16,64,512]{2,1,0:T(8,128)(2,1)}), bf16[16,64,512]{2,1,0:T(8,128)(2,1)S(1)}, u32[]{:S(2)}, u32[]{:S(2)}) async-start(bf16[16,64,512]{2,1,0:T(8,128)(2,1)} %gather_fusion), calls=%async_computation.1 | async-start | bytes 2097152 | tf_op jit(solution)/shard_map/all_to_all | solution.py:65
  44.1 5.1 copy-start.7
  49.1 3.8 copy-start.6
  54.8 5.1 copy-start.7
  59.9 3.8 copy-start.6
  65.6 5.1 copy-start.7
  70.7 3.8 copy-start.6
  76.4 5.1 copy-start.7
  81.5 3.8 copy-start.6
  87.2 5.1 copy-start.7
  92.3 3.8 copy-start.6
  98.0 5.1 copy-start.7
  103.0 3.8 copy-start.6
  108.8 5.1 copy-start.7
  119.6 5.1 copy-start.7
  124.6 27.0 %all-to-all-start.2 = ((f32[16,64,512]{2,1,0:T(8,128)}), f32[16,64,512]{2,1,0:T(8,128)S(1)}, u32[]{:S(2)}, u32[]{:S(2)}) async-start(f32[16,64,512]{2,1,0:T(8,128)} %bitcast.175), calls=%async_computation.2 | async-start | bytes 4194304 | tf_op jit(solution)/shard_map/all_to_all | solution.py:96
  128.4 125.9 %all-reduce.4.cloned.1.call-start = ((), (), s32[]{:S(2)}) async-start(), calls=%async_computation.4 | async-start | bytes 4194304 | tf_op jit(solution)/shard_map/psum | solution.py:107
  155.5 98.8 %copy-start = (f32[1024,512]{1,0:T(8,128)S(1)}, f32[1024,512]{1,0:T(8,128)}, u32[]{:S(2)}) copy-start(f32[1024,512]{1,0:T(8,128)} %param.15) | copy-start | bytes 6291460
  259.3 17.6 %all-to-all-start.3 = ((bf16[16,64,512]{2,1,0:T(8,128)(2,1)}), bf16[16,64,512]{2,1,0:T(8,128)(2,1)}, u32[]{:S(2)}, u32[]{:S(2)}) async-start(bf16[16,64,512]{2,1,0:T(8,128)(2,1)} %gather_fusion.1), calls=%async_computation.3 | async-start | bytes 2097152 | tf_op jit(solution)/shard_map/all_to_all | solution.py:65
  263.7 166.9 %all-reduce.6.cloned.1.call-start = ((), (), s32[]{:S(2)}) async-start(), calls=%async_computation.5 | async-start | bytes 4194304 | tf_op jit(solution)/shard_map/psum | solution.py:122
  370.6 60.0 %copy-start.2 = (f32[1024,512]{1,0:T(8,128)S(1)}, f32[1024,512]{1,0:T(8,128)}, u32[]{:S(2)}) copy-start(f32[1024,512]{1,0:T(8,128)} %param.16) | copy-start | bytes 6291460
  370.6 241.1 %all-reduce.8.cloned.1.call-start = ((), (), s32[]{:S(2)}) async-start(), calls=%async_computation.6 | async-start | bytes 4194304 | tf_op jit(solution)/shard_map/psum | solution.py:133
  441.1 3.8 copy-start.5
  450.4 3.8 copy-start.5
  459.7 3.8 copy-start.5
  469.0 3.8 copy-start.5
  478.4 3.8 copy-start.5
  487.7 3.8 copy-start.5
  497.0 3.8 copy-start.5
  506.4 3.8 copy-start.5
  510.2 101.5 %copy-start.3 = (f32[1024,512]{1,0:T(8,128)S(1)}, f32[1024,512]{1,0:T(8,128)}, u32[]{:S(2)}) copy-start(f32[1024,512]{1,0:T(8,128)} %param.17) | copy-start | bytes 6291460
  (11 other events, 38.6 us)
Sparse Core Ops, SparseCore 0:
  155.6 98.5 all-reduce.3
  370.7 59.7 all-reduce.5
  510.3 101.3 all-reduce.7
where the time goes:
time: 626 us; the launch traced here: 622 us
  waiting for transfers between devices  307 us (49%)
  matrix products  107 us (17%)
  other arithmetic  65.5 us (10%)
  local copies, waits for them, and re-layouts  64.8 us (10%)
  loops' own time  47.1 us (8%)
  starting transfers between devices  16.3 us (3%)
  between operations  13.8 us (2%)
    dot_general x24, matrix products, block_gradient(): jnp.einsum(grad_form, misfit, khatri, preferred_element_type=jnp.float32)  106 us
    psum x1, waiting for transfers between devices, per_device(): third_part = lax.psum(third_part, ('ia', 'ja'))  102 us
    psum x1, waiting for transfers between devices, per_device(): first_part = lax.psum(first_part, ('ja', 'ka'))  98.7 us
    psum x1, waiting for transfers between devices, per_device(): second_part = lax.psum(second_part, ('ia', 'ka'))  59.9 us
    another operation x3, loops' own time, accumulate(): return lax.fori_loop(0, blocks.shape[0], visit, empty)  47.1 us
    convert_element_type x32, local copies, waits for them, and re-layouts, block_gradient(): misfit = (cube.astype(jnp.float32) - model).astype(jnp.bfloat16)  34.5 us
    convert_element_type x24, other arithmetic, block_gradient(): misfit = (cube.astype(jnp.float32) - model).astype(jnp.bfloat16)  26.8 us
    all_to_all x1, waiting for transfers between devices, per_device(): lax.all_to_all(slot_terms.reshape(all_slots, edge, width), 'ia', split_ax...  23.1 us
  transfers between devices with their start and end apart: 7, of which 7 were waited for; matrix products, arithmetic and copies ran while one was open for 1% of the time, Pallas kernels for 0%

commit v1 on v0

--- a/solution.py
+++ b/solution.py
@@ -104,7 +104,8 @@
         precision=lax.Precision.HIGHEST,
         preferred_element_type=jnp.float32,
     ).reshape(span_one, width)
-    first_part = lax.psum(first_part, ("ja", "ka"))
+    shards = lax.all_gather(first_part, ("ja", "ka"), axis=0, tiled=False)
+    first_part = shards.sum(axis=0)
     factor_one = factor_one + STEP_SIZE * first_part
     first_rows = serve_rows(incoming, factor_one, edge, held_rows).reshape(
         groups * per_pair * edge, width

time: 626 us -> 710 us (1.13)
  waiting for transfers between devices: 307 us -> 379 us
  other arithmetic: 65.5 us -> 78.3 us
    all_gather x0 -> x1, waiting for transfers between devices: none -> 169 us  [per_device(): shards = lax.all_gather(first_part, ('ja', 'ka'), axis=0, tiled=False)]
    psum x1 -> x0, waiting for transfers between devices: 98.7 us -> none  [per_device(): first_part = lax.psum(first_part, ('ja', 'ka'))]
    reduce_sum x0 -> x1, other arithmetic: none -> 12.7 us  [per_device(): first_part = shards.sum(axis=0)]
where the time goes in v1:
time: 710 us; the launch traced here: 706 us
  waiting for transfers between devices  379 us (53%)
  matrix products  107 us (15%)
  other arithmetic  78.3 us (11%)
  local copies, waits for them, and re-layouts  64.9 us (9%)
  loops' own time  46.6 us (7%)
  starting transfers between devices  16.3 us (2%)
  between operations  13.8 us (2%)
    all_gather x1, waiting for transfers between devices, per_device(): shards = lax.all_gather(first_part, ('ja', 'ka'), axis=0, tiled=False)  169 us
    dot_general x24, matrix products, block_gradient(): jnp.einsum(grad_form, misfit, khatri, preferred_element_type=jnp.float32)  106 us
    psum x1, waiting for transfers between devices, per_device(): third_part = lax.psum(third_part, ('ia', 'ja'))  102 us
    psum x1, waiting for transfers between devices, per_device(): second_part = lax.psum(second_part, ('ia', 'ka'))  60.9 us
    another operation x3, loops' own time, accumulate(): return lax.fori_loop(0, blocks.shape[0], visit, empty)  46.6 us
    convert_element_type x32, local copies, waits for them, and re-layouts, block_gradient(): misfit = (cube.astype(jnp.float32) - model).astype(jnp.bfloat16)  34.5 us
    convert_element_type x24, other arithmetic, block_gradient(): misfit = (cube.astype(jnp.float32) - model).astype(jnp.bfloat16)  26.8 us
    all_to_all x1, waiting for transfers between devices, per_device(): lax.all_to_all(slot_terms.reshape(all_slots, edge, width), 'ia', split_ax...  23.1 us
  transfers between devices with their start and end apart: 7, of which 7 were waited for; matrix products, arithmetic and copies ran while one was open for 1% of the time, Pallas kernels for 0%

profile of v1, /device:TPU:0, one launch (start us, length us, event | category | flops | bytes accessed | tf_op | source)
XLA Modules:
  0.0 706.1 jit_solution(1299535961271233969)
XLA Ops:
  10.6 4.3 all-to-all-start
  27.9 8.9 %all-to-all-done.1 = bf16[16,64,512]{2,1,0:T(8,128)(2,1)S(1)} async-done(((bf16[16,64,512]{2,1,0:T(8,128)(2,1)}), bf16[16,64,512]{2,1,0:T(8,128)(2,1)S(1)}, u32[]{:S(2)}, u32[]{:S(2)}) %all-to-all-start.1) | async-done | bytes 1048608 | tf_op jit(solution)/shard_map/all_to_all | solution.py:65
  38.3 84.5 %while.40 = (s32[]{:T(128)}, f32[1024,512]{1,0:T(8,128)}, s32[8,3]{0,1:T(4,128)S(1)}, bf16[8,64,4096]{2,1,0:T(8,128)(2,1)}, bf16[1024,512]{1,0:T(8,128)(2,1)S(1)...) while((s32[]{:T(128)}, f32[1024,512]{1,0:T(8,128)}, ...), condition=%wide.region_4.5_spmd, body=%wide.region_3.4_spmd.sunk | while | flops 546144256 | bytes 15402391 | solution.py:49
  43.8 5.0 fusion.118
  54.4 5.0 fusion.118
  65.0 5.0 fusion.118
  75.5 5.0 fusion.118
  86.1 5.0 fusion.118
  96.7 5.0 fusion.118
  107.3 5.0 fusion.118
  117.8 5.0 fusion.118
  126.8 23.1 %all-to-all-done.2 = f32[16,64,512]{2,1,0:T(8,128)S(1)} async-done(((f32[16,64,512]{2,1,0:T(8,128)}), f32[16,64,512]{2,1,0:T(8,128)S(1)}, u32[]{:S(2)}, u32[]{:S(2)}) %all-to-all-start.2) | async-done | bytes 2097184 | tf_op jit(solution)/shard_map/all_to_all | solution.py:96
  153.8 168.5 %all-gather.2.cloned.1.call-done = f32[16,1024,512]{2,1,0:T(8,128)} async-done(((f32[1,1024,512]{2,1,0:T(8,128)}), f32[16,1024,512]{2,1,0:T(8,128)}) %all-gather.2.cloned.1.call-update) | async-done | bytes 33554448 | tf_op jit(solution)/shard_map/all_gather | solution.py:107
  322.3 12.7 %reduce_sum.22 = f32[1024,512]{1,0:T(8,128)S(1)} reduce(f32[16,1024,512]{2,1,0:T(8,128)} %all-gather.2.cloned.1.call-done, f32[]{:T(128)} %constant.179.clone.1), dimensions={0}, to_apply=%region_5.6 | reduce | flops 7864320 | bytes 35651588 | tf_op jit(solution)/shard_map/reduce_sum | solution.py:108
  340.0 4.4 all-to-all-start.3
  344.7 14.1 %all-to-all-done.3 = bf16[16,64,512]{2,1,0:T(8,128)(2,1)} async-done(((bf16[16,64,512]{2,1,0:T(8,128)(2,1)}), bf16[16,64,512]{2,1,0:T(8,128)(2,1)}, u32[]{:S(2)}, u32[]{:S(2)}) %all-to-all-start.3) | async-done | bytes 1048608 | tf_op jit(solution)/shard_map/all_to_all | solution.py:65
  360.4 93.1 %while.41 = (s32[]{:T(128)}, f32[1024,512]{1,0:T(8,128)}, s32[8,3]{0,1:T(4,128)S(1)}, s32[]{:T(128)}, bf16[8,64,4096]{2,1,0:T(8,128)(2,1)}, /*index=5*/s32[]{:T(...) while((s32[]{:T(128)}, f32[1024,512]{1,0:T(8,128)}, ...), condition=%wide.region_7.8_spmd, body=%wide.region_6.7_spmd.sunk | while | flops 546144256 | bytes 9110879 | solution.py:49
  367.7 4.4 fusion.123
  379.3 4.4 fusion.123
  391.0 4.4 fusion.123
  402.6 4.4 fusion.123
  414.2 4.4 fusion.123
  425.9 4.4 fusion.123
  437.5 4.4 fusion.123
  449.2 4.4 fusion.123
  453.6 60.9 %all-reduce.3.cloned.1.call-done = f32[1024,512]{1,0:T(8,128)} async-done(((f32[1024,512]{1,0:T(8,128)}), f32[1024,512]{1,0:T(8,128)}) %all-reduce.3.cloned.1.call-update) | async-done | bytes 2097168 | tf_op jit(solution)/shard_map/psum | solution.py:123
  519.5 75.0 %while.42 = (s32[]{:T(128)}, f32[1024,512]{1,0:T(8,128)}, s32[8,3]{0,1:T(4,128)S(1)}, s32[]{:T(128)}, bf16[8,64,4096]{2,1,0:T(8,128)(2,1)}, /*index=5*/s32[]{:T(...) while((s32[]{:T(128)}, f32[1024,512]{1,0:T(8,128)}, ...), condition=%wide.region_10.11_spmd, body=%wide.region_9.10_spmd.sunk | while | flops 546144256 | bytes 15402391 | solution.py:49
  534.5 3.8 fusion.128
  553.2 3.8 fusion.128
  562.6 3.8 fusion.128
  581.4 3.8 fusion.128
  594.6 101.5 %all-reduce.5.cloned.1.call-done = f32[1024,512]{1,0:T(8,128)} async-done(((f32[1024,512]{1,0:T(8,128)}), f32[1024,512]{1,0:T(8,128)}) %all-reduce.5.cloned.1.call-update) | async-done | bytes 2097168 | tf_op jit(solution)/shard_map/psum | solution.py:134
  (239 shorter events, 156.5 us)
Async XLA Ops:
  10.6 8.0 %all-to-all-start = ((s32[2,8,1]{1,2,0:T(1,128)}), s32[2,8,1]{1,2,0:T(1,128)S(1)}, u32[]{:S(2)}, u32[]{:S(2)}) async-start(s32[2,8,1]{1,2,0:T(1,128)} %bitcast.29), calls=%async_computation | async-start | bytes 2048 | tf_op jit(solution)/shard_map/all_to_all | solution.py:83
  20.3 16.5 %all-to-all-start.1 = ((bf16[16,64,512]{2,1,0:T(8,128)(2,1)}), bf16[16,64,512]{2,1,0:T(8,128)(2,1)S(1)}, u32[]{:S(2)}, u32[]{:S(2)}) async-start(bf16[16,64,512]{2,1,0:T(8,128)(2,1)} %gather_fusion), calls=%async_computation.1 | async-start | bytes 2097152 | tf_op jit(solution)/shard_map/all_to_all | solution.py:65
  43.8 5.1 copy-start.6
  54.4 5.1 copy-start.6
  65.0 5.1 copy-start.6
  75.5 5.1 copy-start.6
  86.1 5.1 copy-start.6
  96.7 5.1 copy-start.6
  107.2 5.1 copy-start.6
  117.8 5.1 copy-start.6
  122.9 27.0 %all-to-all-start.2 = ((f32[16,64,512]{2,1,0:T(8,128)}), f32[16,64,512]{2,1,0:T(8,128)S(1)}, u32[]{:S(2)}, u32[]{:S(2)}) async-start(f32[16,64,512]{2,1,0:T(8,128)} %bitcast.174), calls=%async_computation.2 | async-start | bytes 4194304 | tf_op jit(solution)/shard_map/all_to_all | solution.py:96
  126.6 195.7 %all-gather.2.cloned.1.call-start = ((), (), s32[]{:S(2)}) async-start(), calls=%async_computation.4 | async-start | bytes 35651584 | tf_op jit(solution)/shard_map/all_gather | solution.py:107
  340.0 18.8 %all-to-all-start.3 = ((bf16[16,64,512]{2,1,0:T(8,128)(2,1)}), bf16[16,64,512]{2,1,0:T(8,128)(2,1)}, u32[]{:S(2)}, u32[]{:S(2)}) async-start(bf16[16,64,512]{2,1,0:T(8,128)(2,1)} %gather_fusion.1), calls=%async_computation.3 | async-start | bytes 2097152 | tf_op jit(solution)/shard_map/all_to_all | solution.py:65
  344.5 170.1 %all-reduce.3.cloned.1.call-start = ((), (), s32[]{:S(2)}) async-start(), calls=%async_computation.5 | async-start | bytes 4194304 | tf_op jit(solution)/shard_map/psum | solution.py:123
  453.5 61.0 %copy-start.1 = (f32[1024,512]{1,0:T(8,128)S(1)}, f32[1024,512]{1,0:T(8,128)}, u32[]{:S(2)}) copy-start(f32[1024,512]{1,0:T(8,128)} %param.16) | copy-start | bytes 6291460
  453.6 242.6 %all-reduce.5.cloned.1.call-start = ((), (), s32[]{:S(2)}) async-start(), calls=%async_computation.6 | async-start | bytes 4194304 | tf_op jit(solution)/shard_map/psum | solution.py:134
  525.1 3.8 copy-start.4
  528.9 3.6 copy-start.3
  534.5 3.8 copy-start.4
  538.3 3.6 copy-start.3
  543.8 3.8 copy-start.4
  547.7 3.6 copy-start.3
  553.2 3.8 copy-start.4
  557.1 3.6 copy-start.3
  562.6 3.8 copy-start.4
  566.4 3.6 copy-start.3
  572.0 3.8 copy-start.4
  575.8 3.6 copy-start.3
  581.4 3.8 copy-start.4
  585.2 3.6 copy-start.3
  590.8 3.8 copy-start.4
  594.6 101.6 %copy-start.2 = (f32[1024,512]{1,0:T(8,128)S(1)}, f32[1024,512]{1,0:T(8,128)}, u32[]{:S(2)}) copy-start(f32[1024,512]{1,0:T(8,128)} %param.17) | copy-start | bytes 6291460
  (10 other events, 34.8 us)
Sparse Core Ops, SparseCore 0:
  153.9 168.3 all-gather.1
  453.7 60.8 all-reduce.2
  594.7 101.3 all-reduce.4
